TPU v7x, 128 devices: a whole 4x4x4 slice. The times are simulated.
128 devices in a mesh: dp: 8 (over z_lo, x), seq: 16 (over z_hi, y, core).
Axes of the slice: x: 4, y: 4, z: 4 (z_hi: 2, z_lo: 2; z = z_hi * 2 + z_lo), core: 2. Of those that a mesh axis runs over, the one named last changes fastest.
Arguments:
- series: bfloat16 [8, 8192, 128], P('dp', 'seq'), may hold values from -6 to 6
- cotangent: bfloat16 [8, 8192, 128], P('dp', 'seq'), may hold values from -6 to 6
- w_in: bfloat16 [128, 384], replicated, may hold values from -0.5 to 0.5
- w_out: bfloat16 [128, 128], replicated, may hold values from -0.5 to 0.5
- taps: float32 [3, 384], replicated, may hold values from -3 to 3
- skip_one: float32 [128], replicated, may hold values from 0.5 to 1.5
- skip_two: float32 [128], replicated, may hold values from 0.5 to 1.5
- filter_one: float32 [8, 8192], P(None, 'seq'), may hold values from -0.0625 to 0.0625
- filter_two: float32 [8, 8192], P(None, 'seq'), may hold values from -0.0625 to 0.0625
Outputs:
- output: bfloat16 [8, 8192, 128], P('dp', 'seq')
- d_series: bfloat16 [8, 8192, 128], P('dp', 'seq')
- grad_w_in: float32 [128, 384], replicated
- grad_w_out: float32 [128, 128], replicated
- grad_taps: float32 [3, 384], replicated
- grad_skip_one: float32 [128], replicated
- grad_skip_two: float32 [128], replicated
- grad_filter_one: float32 [8, 8192], P(None, 'seq')
- grad_filter_two: float32 [8, 8192], P(None, 'seq')
All inputs are finite; a program needn't handle non-finite values.
Results may differ from a plain program's by a relative error of at most 0.015.
Values may be sent and summed in bfloat16 or wider, within the bound.
A program may use at most 128 MiB of HBM per device.

v0:
```python
import math
import numpy as np
import jax
import jax.numpy as jnp
from jax import lax
from jax.sharding import PartitionSpec as P

HIGHEST = lax.Precision.HIGHEST
LANES = 128


def dft_tables(length):
    size = 2 * length
    rows = size // LANES
    half = length // LANES
    k1 = np.arange(rows)
    f1 = np.exp(-2j * np.pi * (np.outer(k1, np.arange(half)) % rows) / rows)
    turn = np.exp(-2j * np.pi * np.outer(k1, np.arange(LANES)) / size)
    f2 = np.exp(-2j * np.pi * (np.outer(np.arange(LANES), np.arange(LANES)) % LANES) / LANES)
    fwd1 = np.concatenate([f1.real, f1.imag], axis=0)
    fwd2 = np.block([[f2.real, f2.imag], [-f2.imag, f2.real]])
    inv2 = np.block([[f2.real, -f2.imag], [f2.imag, f2.real]])
    inv1 = np.concatenate([f1.real.T, f1.imag.T], axis=1) / size
    as32 = lambda a: jnp.asarray(np.asarray(a, np.float32))
    return {
        "rows": rows,
        "fwd1": as32(fwd1),
        "fwd2": as32(fwd2),
        "inv1": as32(inv1),
        "inv2": as32(inv2),
        "turn_r": as32(turn.real)[:, None, :],
        "turn_i": as32(turn.imag)[:, None, :],
    }


def spectrum(x, tab):
    rows = tab["rows"]
    a = jnp.einsum("kn,ncm->kcm", tab["fwd1"], x, precision=HIGHEST)
    ar, ai = (a[:rows], a[rows:])
    tr, ti = (tab["turn_r"], tab["turn_i"])
    cat = jnp.concatenate([ar * tr - ai * ti, ar * ti + ai * tr], axis=-1)
    return jnp.einsum("kcm,mj->kcj", cat, tab["fwd2"], precision=HIGHEST)


def signal(s, tab):
    b = jnp.einsum("kcj,jm->kcm", s, tab["inv2"], precision=HIGHEST)
    br, bi = (b[..., :LANES], b[..., LANES:])
    tr, ti = (tab["turn_r"], tab["turn_i"])
    stacked = jnp.concatenate([br * tr + bi * ti, bi * tr - br * ti], axis=0)
    return jnp.einsum("nk,kcm->ncm", tab["inv1"], stacked, precision=HIGHEST)


def cmul(a, b, conj=False):
    ar, ai = (a[..., :LANES], a[..., LANES:])
    br, bi = (b[..., :LANES], b[..., LANES:])
    if conj:
        bi = -bi
    return jnp.concatenate([ar * br - ai * bi, ar * bi + ai * br], axis=-1)


def fold(x):
    c, length = x.shape
    return jnp.swapaxes(x.reshape(c, length // LANES, LANES), 0, 1)


def unfold(x):
    half, c, lanes = x.shape
    return jnp.swapaxes(x, 0, 1).reshape(c, half * lanes)


def shards(series, cotangent, w_in, w_out, taps, skip_one, skip_two, filter_one, filter_two):
    _, block, width = series.shape
    seq_n = lax.axis_size("seq")
    dp_n = lax.axis_size("dp")
    length = block * seq_n
    half = length // LANES
    me = lax.axis_index("seq")
    per = width // seq_n
    filters = filter_one.shape[0]
    group_width = width // filters
    per_group = group_width // per
    group = me // per_group
    grad_scale = 1.0 / math.sqrt(dp_n * series.shape[0] * length)
    tab = dft_tables(length)
    rows_sent = jnp.repeat(
        jnp.swapaxes(jnp.stack([filter_one, filter_two]), 0, 1), per_group, axis=0
    )
    rows_got = lax.all_to_all(rows_sent, "seq", 0, 0, tiled=True)
    h_rows = jnp.swapaxes(rows_got, 0, 1).reshape(2, length)
    taps_sel = lax.dynamic_index_in_dim(
        taps.reshape(3, 3, seq_n, per), me, axis=2, keepdims=False
    ).reshape(3, 3 * per)
    skip1 = lax.dynamic_index_in_dim(skip_one.reshape(seq_n, per), me, axis=0, keepdims=False)
    skip2 = lax.dynamic_index_in_dim(skip_two.reshape(seq_n, per), me, axis=0, keepdims=False)
    skip1 = skip1[None, :, None]
    skip2 = skip2[None, :, None]
    proj_blk = jnp.einsum("td,dc->ct", series[0], w_in, preferred_element_type=jnp.float32)
    proj_blk = lax.all_to_all(proj_blk.reshape(3, seq_n, per, block), "seq", 1, 1, tiled=True)
    proj = jnp.swapaxes(proj_blk, 1, 2).reshape(3 * per, length)
    prev1 = jnp.pad(proj, ((0, 0), (1, 0)))[:, :length]
    prev2 = jnp.pad(proj, ((0, 0), (2, 0)))[:, :length]
    conv = taps_sel[0][:, None] * proj + taps_sel[1][:, None] * prev1 + taps_sel[2][:, None] * prev2
    conv_f = fold(conv)
    value = conv_f[:, :per]
    gate_one = conv_f[:, per : 2 * per]
    gate_two = conv_f[:, 2 * per :]
    h_spec = spectrum(fold(h_rows), tab)
    h_one = h_spec[:, 0:1]
    h_two = h_spec[:, 1:2]
    v_spec = spectrum(value, tab)
    y_one = signal(cmul(v_spec, h_one), tab) + skip1 * value
    gated_mid = gate_one * y_one
    m_spec = spectrum(gated_mid, tab)
    y_two = signal(cmul(m_spec, h_two), tab) + skip2 * gated_mid
    product = (gate_two * y_two).astype(jnp.bfloat16)
    dprod_blk = jnp.einsum("td,cd->ct", cotangent[0], w_out, preferred_element_type=jnp.float32)
    dprod_blk = lax.all_to_all(dprod_blk.reshape(seq_n, per, block), "seq", 0, 0, tiled=True)
    d_product = jnp.swapaxes(dprod_blk.reshape(seq_n, per, block // LANES, LANES), 1, 2).reshape(
        half, per, LANES
    )
    grad_two = d_product * gate_two
    d_gate_two = d_product * y_two
    g2_spec = spectrum(grad_two, tab)
    d_mid = signal(cmul(g2_spec, h_two, conj=True), tab) + skip2 * grad_two
    grad_one = d_mid * gate_one
    d_gate_one = d_mid * y_one
    g1_spec = spectrum(grad_one, tab)
    d_value = signal(cmul(g1_spec, h_one, conj=True), tab) + skip1 * grad_one
    corr = jnp.concatenate(
        [
            jnp.sum(cmul(g1_spec, v_spec, conj=True), axis=1, keepdims=True),
            jnp.sum(cmul(g2_spec, m_spec, conj=True), axis=1, keepdims=True),
        ],
        axis=1,
    )
    filt_grad = unfold(signal(corr, tab))
    d_conv = unfold(jnp.concatenate([d_value, d_gate_one, d_gate_two], axis=1))
    next1 = jnp.pad(d_conv, ((0, 0), (0, 1)))[:, 1:]
    next2 = jnp.pad(d_conv, ((0, 0), (0, 2)))[:, 2:]
    d_proj = (
        taps_sel[0][:, None] * d_conv + taps_sel[1][:, None] * next1 + taps_sel[2][:, None] * next2
    ).astype(jnp.bfloat16)
    local_taps = jnp.stack(
        [
            jnp.sum(d_conv * proj, axis=1),
            jnp.sum(d_conv * prev1, axis=1),
            jnp.sum(d_conv * prev2, axis=1),
        ]
    )
    local_skip1 = jnp.sum(grad_one * value, axis=(0, 2))
    local_skip2 = jnp.sum(grad_two * gated_mid, axis=(0, 2))
    prod_blocks = product.reshape(seq_n, half // seq_n, per, LANES)
    prod_blocks = lax.all_to_all(prod_blocks, "seq", 0, 0, tiled=True)
    output = jnp.einsum(
        "jnim,jid->nmd",
        prod_blocks,
        w_out.reshape(seq_n, per, width),
        preferred_element_type=jnp.float32,
    ).astype(jnp.bfloat16)
    output = output.reshape(1, block, width)
    dp_blocks = d_proj.reshape(3, per, seq_n, block)
    dp_blocks = lax.all_to_all(dp_blocks, "seq", 2, 2, tiled=True)
    d_series = jnp.einsum(
        "pijt,dpji->td",
        dp_blocks,
        w_in.reshape(width, 3, seq_n, per),
        preferred_element_type=jnp.float32,
    ).astype(jnp.bfloat16)
    d_series = d_series.reshape(1, block, width)
    fg_blocks = lax.all_to_all(filt_grad.reshape(2, seq_n, block), "seq", 1, 1, tiled=True)
    fg_blocks = jnp.sum(fg_blocks.reshape(2, filters, per_group, block), axis=2)
    prod_rows = jnp.transpose(prod_blocks, (1, 3, 0, 2)).reshape(block, width)
    dp_rows = jnp.transpose(dp_blocks, (3, 0, 2, 1)).reshape(block, 3 * width)
    local_w_in = jnp.einsum("td,tc->dc", series[0], dp_rows, preferred_element_type=jnp.float32)
    local_w_out = jnp.einsum(
        "tc,td->cd", prod_rows, cotangent[0], preferred_element_type=jnp.float32
    )
    small = jnp.concatenate(
        [
            local_taps.reshape(3, 3, 1, per),
            jnp.stack([local_skip1, local_skip2, jnp.zeros_like(local_skip1)]).reshape(
                3, 1, 1, per
            ),
        ],
        axis=1,
    )
    small_full = jnp.zeros((3, 4, seq_n, per), jnp.float32)
    small_full = lax.dynamic_update_slice(small_full, small, (0, 0, me, 0))
    grad_w_in, grad_w_out, small_full = lax.psum(
        (local_w_in, local_w_out, small_full), ("dp", "seq")
    )
    fg_blocks = lax.psum(fg_blocks, "dp")
    small_full = small_full.reshape(3, 4, width)
    grad_taps = small_full[:, :3].reshape(3, 3 * width)
    grad_skip_one = small_full[0, 3]
    grad_skip_two = small_full[1, 3]
    return (
        output,
        d_series,
        grad_scale * grad_w_in,
        grad_scale * grad_w_out,
        grad_scale * grad_taps,
        grad_scale * grad_skip_one,
        grad_scale * grad_skip_two,
        grad_scale * fg_blocks[0],
        grad_scale * fg_blocks[1],
    )


def solution(mesh):
    in_specs = (
        P("dp", "seq", None),
        P("dp", "seq", None),
        P(),
        P(),
        P(),
        P(),
        P(),
        P(None, "seq"),
        P(None, "seq"),
    )
    out_specs = (
        P("dp", "seq", None),
        P("dp", "seq", None),
        P(),
        P(),
        P(),
        P(),
        P(),
        P(None, "seq"),
        P(None, "seq"),
    )
    return jax.shard_map(shards, mesh=mesh, in_specs=in_specs, out_specs=out_specs, check_vma=False)
```

profile of v0, /device:TPU:1, one launch (start us, length us, event | category | flops | bytes accessed | tf_op | source)
XLA Modules:
  0.0 364.3 jit_solution(12172871343249868817)
XLA Ops:
  7.2 0.8 maximum_bitcast_fusion
  8.0 0.6 broadcast_in_dim.16
  8.6 9.4 %all-to-all-start.1 = ((f32[16,2,512]{2,1,0:T(2,128)}), f32[16,2,512]{2,1,0:T(2,128)S(1)}, u32[]{:S(2)}, u32[]{:S(2)}) async-start(f32[16,2,512]{2,1,0:T(2,128)} %bitcast.12), calls=%async_computation.1 | async-start | bytes 131072 | tf_op jit(solution)/shard_map/all_to_all | solution.py:88
  18.1 0.7 copy-done.11
  19.3 0.5 copy-done.12
  19.9 0.6 copy-done.13
  20.6 1.2 fusion.68
  21.8 0.9 fusion.70
  22.7 2.7 all-to-all-done.1
  25.4 4.6 %all-to-all-start.3 = ((f32[16,8,512]{2,1,0:T(8,128)}), f32[16,8,512]{2,1,0:T(8,128)S(1)}, u32[]{:S(2)}, u32[]{:S(2)}) async-start(f32[16,8,512]{2,1,0:T(8,128)} %fusion.70), calls=%async_computation.3 | async-start | bytes 524288 | tf_op jit(solution)/shard_map/all_to_all | solution.py:117
  30.0 0.8 copy-done.6
  30.8 0.4 fusion.76
  31.3 0.4 copy-done.3
  31.8 6.9 %all-to-all-done.3 = f32[16,8,512]{2,1,0:T(8,128)S(1)} async-done(((f32[16,8,512]{2,1,0:T(8,128)}), f32[16,8,512]{2,1,0:T(8,128)S(1)}, u32[]{:S(2)}, u32[]{:S(2)}) %all-to-all-start.3) | async-done | bytes 262176 | tf_op jit(solution)/shard_map/all_to_all | solution.py:117
  38.7 4.2 %all-to-all-start = ((f32[3,16,8,512]{3,2,0,1:T(8,128)}), f32[3,16,8,512]{3,2,0,1:T(8,128)S(1)}, u32[]{:S(2)}, u32[]{:S(2)}) async-start(f32[3,16,8,512]{3,2,0,1:T(8,128)} %fusion.68), calls=%async_computation | async-start | bytes 1572864 | tf_op jit(solution)/shard_map/all_to_all | solution.py:98
  42.9 0.6 fusion.53
  43.6 13.9 %all-to-all-done = f32[3,16,8,512]{3,2,0,1:T(8,128)S(1)} async-done(((f32[3,16,8,512]{3,2,0,1:T(8,128)}), f32[3,16,8,512]{3,2,0,1:T(8,128)S(1)}, u32[]{:S(2)}, u32[]{:S(2)}) %all-to-all-start) | async-done | bytes 786464 | tf_op jit(solution)/shard_map/all_to_all | solution.py:98
  57.5 0.5 copy.253
  58.0 0.5 copy.221
  58.5 0.5 add_bitcast_fusion
  59.1 1.0 fusion.64
  60.2 1.0 fusion.102
  61.3 1.9 fusion.25
  63.3 0.8 copy-done.1
  64.1 1.1 fusion.29
  65.4 0.7 copy-done.5
  66.1 1.1 convolution_add_fusion.1
  67.3 1.0 fusion.101
  68.5 1.9 fusion.3
  70.4 2.0 fusion.36
  72.4 0.4 multiply_subtract_fusion.1
  72.9 1.1 fusion.7
  74.0 1.1 fusion.40
  75.4 1.1 convolution_add_fusion.3
  76.5 1.0 fusion.100
  77.7 1.9 fusion.14
  79.8 1.1 fusion.18
  81.1 1.1 convolution_add_fusion
  82.2 1.2 multiply_reduce_fusion.3
  83.5 0.6 multiply_reduce_fusion.1
  84.1 0.7 copy.248
  84.9 0.6 fusion.57
  86.0 0.7 copy.198
  86.7 4.0 %all-to-all-start.5 = ((f32[2,16,512]{2,0,1:T(2,128)}), f32[2,16,512]{2,0,1:T(2,128)S(1)}, u32[]{:S(2)}, u32[]{:S(2)}) async-start(f32[2,16,512]{2,0,1:T(2,128)} %copy.198), calls=%async_computation.5 | async-start | bytes 131072 | tf_op jit(solution)/shard_map/all_to_all | solution.py:170
  91.5 67.0 %psum.30 = f32[3,4,128]{2,1,0:T(4,128)S(1)} all-reduce(f32[3,4,128]{2,1,0:T(4,128)S(1)} %reshape.136), channel_id=1, replica_groups=mesh['dp'=8,'seq'=16] {'dp','seq'}, use_global_device_ids=true, to_apply=%region_7.8 | all-reduce | flops 1536 | bytes 12288 | tf_op jit(solution)/shard_map/psum | solution.py:189
  158.5 0.5 fusion.50
  159.0 0.5 fusion.83
  159.5 0.6 copy.252
  160.2 1.0 copy.188
  161.2 0.7 copy.177
  161.9 4.3 %all-to-all-start.2 = ((bf16[16,4,8,128]{3,2,1,0:T(8,128)(2,1)}), bf16[16,4,8,128]{3,2,1,0:T(8,128)(2,1)S(1)}, u32[]{:S(2)}, u32[]{:S(2)}) async-start(bf16[16,4,8,128]{3,2,1,0:T(8,128)(2,1)} %copy.177), calls=%async_computation.2 | async-start | bytes 262144 | tf_op jit(solution)/shard_map/all_to_all | solution.py:153
  166.3 25.2 %psum.31 = f32[2,8,512]{2,0,1:T(2,128)S(1)} all-reduce(f32[2,8,512]{2,0,1:T(2,128)S(1)} %bitcast_reduce_fusion), channel_id=1, replica_groups=mesh['dp'=8,'seq'=16] {'dp'}, use_global_device_ids=true, to_apply=%region_11.12 | all-reduce | flops 8192 | bytes 65536 | tf_op jit(solution)/shard_map/psum | solution.py:192
  191.5 0.6 copy.250
  192.1 0.6 copy.251
  192.7 14.6 %all-to-all-start.4 = ((bf16[3,8,16,512]{3,1,0,2:T(8,128)(2,1)}), bf16[3,8,16,512]{3,1,0,2:T(8,128)(2,1)S(1)}, u32[]{:S(2)}, u32[]{:S(2)}) async-start(bf16[3,8,16,512]{3,1,0,2:T(8,128)(2,1)} %copy.188), calls=%async_computation.4 | async-start | bytes 786432 | tf_op jit(solution)/shard_map/all_to_all | solution.py:162
  207.3 0.9 fusion
  208.2 0.8 fusion.66
  209.0 8.0 %all-to-all-done.4 = bf16[3,8,16,512]{3,1,0,2:T(8,128)(2,1)S(1)} async-done(((bf16[3,8,16,512]{3,1,0,2:T(8,128)(2,1)}), bf16[3,8,16,512]{3,1,0,2:T(8,128)(2,1)S(1)}, u32[]{:S(2)}, u32[]{:S(2)}) %all-to-all-start.4) | async-done | bytes 393248 | tf_op jit(solution)/shard_map/all_to_all | solution.py:162
  217.1 0.9 convolution_bitcast_fusion.2
  218.1 1.0 fusion.2
  219.0 136.0 %all-reduce.7.cloned.1.call-done = (f32[128,384]{0,1:T(8,128)}, f32[128,128]{1,0:T(8,128)}) async-done(((f32[128,384]{0,1:T(8,128)}, f32[128,128]{1,0:T(8,128)}), (f32[128,384]{0,1:T(8,128)}, f32[128,128]{1,0:T(8,128)})) %all-reduce.7.cloned.1.call-update) | async-done | bytes 262160 | tf_op jit(solution)/shard_map/psum | solution.py:189
  355.0 0.9 broadcast_multiply_fusion
  356.0 0.8 copy.199
  356.8 0.6 broadcast_multiply_fusion.1
  (73 shorter events, 4.1 us)
Async XLA Ops:
  7.2 13.4 %copy-start = (bf16[1,512,128]{2,1,0:T(8,128)(2,1)S(1)}, bf16[1,512,128]{2,1,0:T(8,128)(2,1)}, u32[]{:S(2)}) copy-start(bf16[1,512,128]{2,1,0:T(8,128)(2,1)} %param.15) | copy-start | bytes 393220
  8.6 10.5 %copy-start.8 = (bf16[128,384]{1,0:T(8,128)(2,1)S(1)}, bf16[128,384]{1,0:T(8,128)(2,1)}, u32[]{:S(2)}) copy-start(bf16[128,384]{1,0:T(8,128)(2,1)} %param.17) | copy-start | bytes 294916
  8.6 16.8 %all-to-all-start.1 = ((f32[16,2,512]{2,1,0:T(2,128)}), f32[16,2,512]{2,1,0:T(2,128)S(1)}, u32[]{:S(2)}, u32[]{:S(2)}) async-start(f32[16,2,512]{2,1,0:T(2,128)} %bitcast.12), calls=%async_computation.1 | async-start | bytes 131072 | tf_op jit(solution)/shard_map/all_to_all | solution.py:88
  18.1 0.7 copy-start.11
  19.2 0.7 copy-start.12
  19.8 0.7 copy-start.13
  20.6 1.2 copy-start.7
  20.6 1.2 copy-start.10
  25.4 13.3 %all-to-all-start.3 = ((f32[16,8,512]{2,1,0:T(8,128)}), f32[16,8,512]{2,1,0:T(8,128)S(1)}, u32[]{:S(2)}, u32[]{:S(2)}) async-start(f32[16,8,512]{2,1,0:T(8,128)} %fusion.70), calls=%async_computation.3 | async-start | bytes 524288 | tf_op jit(solution)/shard_map/all_to_all | solution.py:117
  30.0 0.8 copy-start.6
  30.8 0.8 copy-start.3
  30.8 0.9 copy-start.4
  31.7 11.1 %copy-start.2 = (f32[256,256,1]{1,0,2:T(8,128)S(1)}, f32[256,256,1]{1,0,2:T(8,128)}, u32[]{:S(2)}) copy-start(f32[256,256,1]{1,0,2:T(8,128)} %constant.59) | copy-start | bytes 786436
  38.7 18.8 %all-to-all-start = ((f32[3,16,8,512]{3,2,0,1:T(8,128)}), f32[3,16,8,512]{3,2,0,1:T(8,128)S(1)}, u32[]{:S(2)}, u32[]{:S(2)}) async-start(f32[3,16,8,512]{3,2,0,1:T(8,128)} %fusion.68), calls=%async_computation | async-start | bytes 1572864 | tf_op jit(solution)/shard_map/all_to_all | solution.py:98
  63.2 1.0 copy-start.1
  65.3 0.8 copy-start.5
  86.7 75.3 %all-to-all-start.5 = ((f32[2,16,512]{2,0,1:T(2,128)}), f32[2,16,512]{2,0,1:T(2,128)S(1)}, u32[]{:S(2)}, u32[]{:S(2)}) async-start(f32[2,16,512]{2,0,1:T(2,128)} %copy.198), calls=%async_computation.5 | async-start | bytes 131072 | tf_op jit(solution)/shard_map/all_to_all | solution.py:170
  161.9 30.8 %all-to-all-start.2 = ((bf16[16,4,8,128]{3,2,1,0:T(8,128)(2,1)}), bf16[16,4,8,128]{3,2,1,0:T(8,128)(2,1)S(1)}, u32[]{:S(2)}, u32[]{:S(2)}) async-start(bf16[16,4,8,128]{3,2,1,0:T(8,128)(2,1)} %copy.177), calls=%async_computation.2 | async-start | bytes 262144 | tf_op jit(solution)/shard_map/all_to_all | solution.py:153
  192.7 24.4 %all-to-all-start.4 = ((bf16[3,8,16,512]{3,1,0,2:T(8,128)(2,1)}), bf16[3,8,16,512]{3,1,0,2:T(8,128)(2,1)S(1)}, u32[]{:S(2)}, u32[]{:S(2)}) async-start(bf16[3,8,16,512]{3,1,0,2:T(8,128)(2,1)} %copy.188), calls=%async_computation.4 | async-start | bytes 786432 | tf_op jit(solution)/shard_map/all_to_all | solution.py:162
  207.3 147.7 %all-reduce.7.cloned.1.call-start = ((), (), s32[]{:S(2)}) async-start(), calls=%async_computation.6 | async-start | bytes 524288 | tf_op jit(solution)/shard_map/psum | solution.py:189
  356.0 0.8 copy-start.9
Sparse Core Ops, SparseCore 0:
  218.2 136.7 all-reduce.6
where the time goes:
time: 365 us; the launch traced here: 364 us
  waiting for transfers between devices  168 us (46%)
  blocking collectives  92.2 us (25%)
  starting transfers between devices  41.2 us (11%)
  matrix products  28.5 us (8%)
  between operations  14.5 us (4%)
  local copies, waits for them, and re-layouts  13.5 us (4%)
  other arithmetic  6.89 us (2%)
    psum x1, waiting for transfers between devices, shards(): lax.psum((local_w_in, local_w_out, small_full), ('dp', 'seq'))  136 us
    psum x1, blocking collectives, shards(): lax.psum((local_w_in, local_w_out, small_full), ('dp', 'seq'))  67 us
    psum x1, blocking collectives, shards(): fg_blocks = lax.psum(fg_blocks, 'dp')  25.2 us
    all_to_all x1, starting transfers between devices, shards(): dp_blocks = lax.all_to_all(dp_blocks, 'seq', 2, 2, tiled=True)  14.6 us
    all_to_all x1, waiting for transfers between devices, shards(): lax.all_to_all(proj_blk.reshape(3, seq_n, per, block), 'seq', 1, 1, tiled...  13.9 us
    all_to_all x1, starting transfers between devices, shards(): rows_got = lax.all_to_all(rows_sent, 'seq', 0, 0, tiled=True)  9.43 us
    unnamed x37, local copies, waits for them, and re-layouts  8.79 us
    dot_general x5, matrix products, spectrum(): return jnp.einsum('kcm,mj->kcj', cat, tab['fwd2'], precision=HIGHEST)  8.23 us
  transfers between devices with their start and end apart: 7, of which 5 were waited for; matrix products, arithmetic and copies ran while one was open for 3% of the time, Pallas kernels for 0%

commit v1 on v0

--- a/solution.py
+++ b/solution.py
@@ -7,6 +7,10 @@
 
 HIGHEST = lax.Precision.HIGHEST
 LANES = 128
+
+
+def try_all_points_now(array_here):
+    return lax.psum(lax.psum(array_here, "dp"), "seq")
 
 
 def dft_tables(length):
@@ -186,9 +190,7 @@
     )
     small_full = jnp.zeros((3, 4, seq_n, per), jnp.float32)
     small_full = lax.dynamic_update_slice(small_full, small, (0, 0, me, 0))
-    grad_w_in, grad_w_out, small_full = lax.psum(
-        (local_w_in, local_w_out, small_full), ("dp", "seq")
-    )
+    grad_w_in, grad_w_out, small_full = try_all_points_now((local_w_in, local_w_out, small_full))
     fg_blocks = lax.psum(fg_blocks, "dp")
     small_full = small_full.reshape(3, 4, width)
     grad_taps = small_full[:, :3].reshape(3, 3 * width)

time: 365 us -> 406 us (1.11)
  waiting for transfers between devices: 168 us -> 242 us
  blocking collectives: 92.2 us -> 69.2 us
  starting transfers between devices: 41.2 us -> 31.1 us
    psum x1 -> x2, waiting for transfers between devices: 136 us -> 205 us  [try_all_points_now(): return lax.psum(lax.psum(array_here, 'dp'), 'seq')]
    psum x2, blocking collectives: 92.2 us -> 69.2 us  [try_all_points_now(): return lax.psum(lax.psum(array_here, 'dp'), 'seq')]
    all_to_all x1, starting transfers between devices: 14.6 us -> 5.08 us  [shards(): dp_blocks = lax.all_to_all(dp_blocks, 'seq', 2, 2, tiled=True)]
    all_to_all x1, waiting for transfers between devices: 0.01 us -> 4.39 us  [shards(): lax.all_to_all(filt_grad.reshape(2, seq_n, block), 'seq', 1, 1, tiled=True)]
  transfers between devices with their start and end apart: 7 -> 8, of which waited for: 5 -> 7; matrix products, arithmetic and copies ran while one was open for 3% -> 3% of each run, Pallas kernels for 0% -> 0%
where the time goes in v1:
time: 406 us; the launch traced here: 405 us
  waiting for transfers between devices  242 us (60%)
  blocking collectives  69.2 us (17%)
  starting transfers between devices  31.1 us (8%)
  matrix products  28.5 us (7%)
  between operations  14.6 us (4%)
  local copies, waits for them, and re-layouts  13.5 us (3%)
  other arithmetic  6.89 us (2%)
    psum x2, waiting for transfers between devices, try_all_points_now(): return lax.psum(lax.psum(array_here, 'dp'), 'seq')  205 us
    psum x2, blocking collectives, try_all_points_now(): return lax.psum(lax.psum(array_here, 'dp'), 'seq')  69.2 us
    all_to_all x1, waiting for transfers between devices, shards(): lax.all_to_all(proj_blk.reshape(3, seq_n, per, block), 'seq', 1, 1, tiled...  13.9 us
    all_to_all x1, starting transfers between devices, shards(): rows_got = lax.all_to_all(rows_sent, 'seq', 0, 0, tiled=True)  9.43 us
    all_to_all x1, waiting for transfers between devices, shards(): dp_blocks = lax.all_to_all(dp_blocks, 'seq', 2, 2, tiled=True)  8.91 us
    unnamed x37, local copies, waits for them, and re-layouts  8.79 us
    dot_general x5, matrix products, spectrum(): return jnp.einsum('kcm,mj->kcj', cat, tab['fwd2'], precision=HIGHEST)  8.23 us
  transfers between devices with their start and end apart: 8, of which 7 were waited for; matrix products, arithmetic and copies ran while one was open for 3% of the time, Pallas kernels for 0%

profile of v1, /device:TPU:1, one launch (start us, length us, event | category | flops | bytes accessed | tf_op | source)
XLA Modules:
  0.0 405.4 jit_solution(9546061533142303671)
XLA Ops:
  7.2 0.8 maximum_bitcast_fusion
  8.0 0.6 broadcast_in_dim.16
  8.6 9.4 %all-to-all-start.1 = ((f32[16,2,512]{2,1,0:T(2,128)}), f32[16,2,512]{2,1,0:T(2,128)S(1)}, u32[]{:S(2)}, u32[]{:S(2)}) async-start(f32[16,2,512]{2,1,0:T(2,128)} %bitcast.12), calls=%async_computation.1 | async-start | bytes 131072 | tf_op jit(solution)/shard_map/all_to_all | solution.py:92
  18.1 0.7 copy-done.11
  19.3 0.5 copy-done.12
  19.9 0.6 copy-done.13
  20.6 1.2 fusion.68
  21.8 0.9 fusion.70
  22.7 2.7 all-to-all-done.1
  25.4 4.6 %all-to-all-start.3 = ((f32[16,8,512]{2,1,0:T(8,128)}), f32[16,8,512]{2,1,0:T(8,128)S(1)}, u32[]{:S(2)}, u32[]{:S(2)}) async-start(f32[16,8,512]{2,1,0:T(8,128)} %fusion.70), calls=%async_computation.3 | async-start | bytes 524288 | tf_op jit(solution)/shard_map/all_to_all | solution.py:121
  30.0 0.8 copy-done.6
  30.8 0.4 fusion.76
  31.8 6.9 %all-to-all-done.3 = f32[16,8,512]{2,1,0:T(8,128)S(1)} async-done(((f32[16,8,512]{2,1,0:T(8,128)}), f32[16,8,512]{2,1,0:T(8,128)S(1)}, u32[]{:S(2)}, u32[]{:S(2)}) %all-to-all-start.3) | async-done | bytes 262176 | tf_op jit(solution)/shard_map/all_to_all | solution.py:121
  38.7 4.2 %all-to-all-start = ((f32[3,16,8,512]{3,2,0,1:T(8,128)}), f32[3,16,8,512]{3,2,0,1:T(8,128)S(1)}, u32[]{:S(2)}, u32[]{:S(2)}) async-start(f32[3,16,8,512]{3,2,0,1:T(8,128)} %fusion.68), calls=%async_computation | async-start | bytes 1572864 | tf_op jit(solution)/shard_map/all_to_all | solution.py:102
  42.9 0.6 fusion.53
  43.6 13.9 %all-to-all-done = f32[3,16,8,512]{3,2,0,1:T(8,128)S(1)} async-done(((f32[3,16,8,512]{3,2,0,1:T(8,128)}), f32[3,16,8,512]{3,2,0,1:T(8,128)S(1)}, u32[]{:S(2)}, u32[]{:S(2)}) %all-to-all-start) | async-done | bytes 786464 | tf_op jit(solution)/shard_map/all_to_all | solution.py:102
  57.5 0.5 copy.253
  58.0 0.5 copy.221
  58.5 0.5 add_bitcast_fusion
  59.1 1.0 fusion.64
  60.2 1.0 fusion.102
  61.3 1.9 fusion.25
  63.3 0.8 copy-done.1
  64.1 1.1 fusion.29
  65.4 0.7 copy-done.5
  66.1 1.1 convolution_add_fusion.1
  67.3 1.0 fusion.101
  68.5 1.9 fusion.3
  70.4 2.0 fusion.36
  72.9 1.1 fusion.7
  74.0 1.1 fusion.40
  75.4 1.1 convolution_add_fusion.3
  76.5 1.0 fusion.100
  77.7 1.9 fusion.14
  79.8 1.1 fusion.18
  81.1 1.1 convolution_add_fusion
  82.2 1.2 multiply_reduce_fusion.3
  83.5 0.6 multiply_reduce_fusion.1
  84.1 0.7 copy.248
  84.9 0.6 fusion.57
  86.0 0.7 copy.198
  86.7 4.0 all-to-all-start.5
  91.3 0.5 fusion.50
  91.9 1.0 copy.188
  92.9 0.7 copy.177
  93.7 4.4 %all-to-all-done.5 = f32[2,16,512]{2,0,1:T(2,128)S(1)} async-done(((f32[2,16,512]{2,0,1:T(2,128)}), f32[2,16,512]{2,0,1:T(2,128)S(1)}, u32[]{:S(2)}, u32[]{:S(2)}) %all-to-all-start.5) | async-done | bytes 65568 | tf_op jit(solution)/shard_map/all_to_all | solution.py:174
  98.1 3.7 all-to-all-start.2
  101.8 28.1 %all-reduce.5 = (f32[3,4,16,8]{3,2,1,0:T(8,128)S(1)}, f32[2,8,512]{2,0,1:T(2,128)S(1)}) all-reduce(f32[3,4,16,8]{3,2,1,0:T(8,128)S(1)} %dynamic_update_slice.3, f32[2,8,512]{2,0,1:T(2,128)S(1)} %bitcast_reduce_fusion), channel_id=1, replica_groups=mesh['dp'=8,'seq'=16] {'dp'}, use_global_device_ids=true, to_apply=%region_9.10 | all-reduce | flops 9728 | bytes 77824 | tf_op jit(solution)/shard_map/psum | solution.py:13
  130.0 41.2 %psum.54 = f32[3,4,128]{2,1,0:T(4,128)S(1)} all-reduce(f32[3,4,128]{2,1,0:T(4,128)S(1)} %reshape.136), channel_id=1, replica_groups=mesh['dp'=8,'seq'=16] {'seq'}, use_global_device_ids=true, to_apply=%region_10.11 | all-reduce | flops 1536 | bytes 12288 | tf_op jit(solution)/shard_map/psum | solution.py:13
  171.2 5.1 %all-to-all-start.4 = ((bf16[3,8,16,512]{3,1,0,2:T(8,128)(2,1)}), bf16[3,8,16,512]{3,1,0,2:T(8,128)(2,1)S(1)}, u32[]{:S(2)}, u32[]{:S(2)}) async-start(bf16[3,8,16,512]{3,1,0,2:T(8,128)(2,1)} %copy.188), calls=%async_computation.4 | async-start | bytes 786432 | tf_op jit(solution)/shard_map/all_to_all | solution.py:166
  176.4 0.8 fusion.66
  177.2 8.9 %all-to-all-done.4 = bf16[3,8,16,512]{3,1,0,2:T(8,128)(2,1)S(1)} async-done(((bf16[3,8,16,512]{3,1,0,2:T(8,128)(2,1)}), bf16[3,8,16,512]{3,1,0,2:T(8,128)(2,1)S(1)}, u32[]{:S(2)}, u32[]{:S(2)}) %all-to-all-start.4) | async-done | bytes 393248 | tf_op jit(solution)/shard_map/all_to_all | solution.py:166
  186.1 0.9 convolution_bitcast_fusion.2
  187.1 0.5 fusion.83
  187.7 0.6 copy.250
  188.3 0.6 copy.251
  188.9 0.6 copy.252
  189.5 0.9 fusion
  190.4 60.9 %all-reduce.12.cloned.1.call-done = (f32[128,384]{0,1:T(8,128)}, f32[128,128]{1,0:T(8,128)}) async-done(((f32[128,384]{0,1:T(8,128)}, f32[128,128]{1,0:T(8,128)}), (f32[128,384]{0,1:T(8,128)}, f32[128,128]{1,0:T(8,128)})) %all-reduce.12.cloned.1.call-update) | async-done | bytes 262160 | tf_op jit(solution)/shard_map/psum | solution.py:13
  251.2 1.0 fusion.2
  252.2 143.9 %all-reduce.10.cloned.1.call-done = (f32[128,384]{0,1:T(8,128)}, f32[128,128]{1,0:T(8,128)}) async-done(((f32[128,384]{0,1:T(8,128)}, f32[128,128]{1,0:T(8,128)}), (f32[128,384]{0,1:T(8,128)}, f32[128,128]{1,0:T(8,128)})) %all-reduce.10.cloned.1.call-update) | async-done | bytes 262160 | tf_op jit(solution)/shard_map/psum | solution.py:13
  396.1 0.9 broadcast_multiply_fusion
  397.1 0.8 copy.199
  397.9 0.6 broadcast_multiply_fusion.1
  (76 shorter events, 5.0 us)
Async XLA Ops:
  7.2 13.4 %copy-start = (bf16[1,512,128]{2,1,0:T(8,128)(2,1)S(1)}, bf16[1,512,128]{2,1,0:T(8,128)(2,1)}, u32[]{:S(2)}) copy-start(bf16[1,512,128]{2,1,0:T(8,128)(2,1)} %param.15) | copy-start | bytes 393220
  8.6 10.5 %copy-start.8 = (bf16[128,384]{1,0:T(8,128)(2,1)S(1)}, bf16[128,384]{1,0:T(8,128)(2,1)}, u32[]{:S(2)}) copy-start(bf16[128,384]{1,0:T(8,128)(2,1)} %param.17) | copy-start | bytes 294916
  8.6 16.8 %all-to-all-start.1 = ((f32[16,2,512]{2,1,0:T(2,128)}), f32[16,2,512]{2,1,0:T(2,128)S(1)}, u32[]{:S(2)}, u32[]{:S(2)}) async-start(f32[16,2,512]{2,1,0:T(2,128)} %bitcast.12), calls=%async_computation.1 | async-start | bytes 131072 | tf_op jit(solution)/shard_map/all_to_all | solution.py:92
  18.1 0.7 copy-start.11
  19.2 0.7 copy-start.12
  19.8 0.7 copy-start.13
  20.6 1.2 copy-start.7
  20.6 1.2 copy-start.10
  25.4 13.3 %all-to-all-start.3 = ((f32[16,8,512]{2,1,0:T(8,128)}), f32[16,8,512]{2,1,0:T(8,128)S(1)}, u32[]{:S(2)}, u32[]{:S(2)}) async-start(f32[16,8,512]{2,1,0:T(8,128)} %fusion.70), calls=%async_computation.3 | async-start | bytes 524288 | tf_op jit(solution)/shard_map/all_to_all | solution.py:121
  30.0 0.8 copy-start.6
  30.8 0.8 copy-start.3
  30.8 0.9 copy-start.4
  31.8 11.1 %copy-start.2 = (f32[256,256,1]{1,0,2:T(8,128)S(1)}, f32[256,256,1]{1,0,2:T(8,128)}, u32[]{:S(2)}) copy-start(f32[256,256,1]{1,0,2:T(8,128)} %constant.59) | copy-start | bytes 786436
  38.7 18.8 %all-to-all-start = ((f32[3,16,8,512]{3,2,0,1:T(8,128)}), f32[3,16,8,512]{3,2,0,1:T(8,128)S(1)}, u32[]{:S(2)}, u32[]{:S(2)}) async-start(f32[3,16,8,512]{3,2,0,1:T(8,128)} %fusion.68), calls=%async_computation | async-start | bytes 1572864 | tf_op jit(solution)/shard_map/all_to_all | solution.py:102
  63.2 1.0 copy-start.1
  65.3 0.8 copy-start.5
  86.7 11.4 %all-to-all-start.5 = ((f32[2,16,512]{2,0,1:T(2,128)}), f32[2,16,512]{2,0,1:T(2,128)S(1)}, u32[]{:S(2)}, u32[]{:S(2)}) async-start(f32[2,16,512]{2,0,1:T(2,128)} %copy.198), calls=%async_computation.5 | async-start | bytes 131072 | tf_op jit(solution)/shard_map/all_to_all | solution.py:174
  98.1 73.1 %all-to-all-start.2 = ((bf16[16,4,8,128]{3,2,1,0:T(8,128)(2,1)}), bf16[16,4,8,128]{3,2,1,0:T(8,128)(2,1)S(1)}, u32[]{:S(2)}, u32[]{:S(2)}) async-start(bf16[16,4,8,128]{3,2,1,0:T(8,128)(2,1)} %copy.177), calls=%async_computation.2 | async-start | bytes 262144 | tf_op jit(solution)/shard_map/all_to_all | solution.py:157
  171.2 14.9 %all-to-all-start.4 = ((bf16[3,8,16,512]{3,1,0,2:T(8,128)(2,1)}), bf16[3,8,16,512]{3,1,0,2:T(8,128)(2,1)S(1)}, u32[]{:S(2)}, u32[]{:S(2)}) async-start(bf16[3,8,16,512]{3,1,0,2:T(8,128)(2,1)} %copy.188), calls=%async_computation.4 | async-start | bytes 786432 | tf_op jit(solution)/shard_map/all_to_all | solution.py:166
  176.3 74.9 %all-reduce.12.cloned.1.call-start = ((), (), s32[]{:S(2)}) async-start(), calls=%async_computation.7 | async-start | bytes 524288 | tf_op jit(solution)/shard_map/psum | solution.py:13
  187.1 209.0 %all-reduce.10.cloned.1.call-start = ((), (), s32[]{:S(2)}) async-start(), calls=%async_computation.6 | async-start | bytes 524288 | tf_op jit(solution)/shard_map/psum | solution.py:13
  397.0 0.8 copy-start.9
Sparse Core Ops, SparseCore 0:
  187.2 63.9 all-reduce.11
  253.9 142.1 all-reduce.9
